TPU v7x, 256 devices: a whole 4x4x8 slice. The times are simulated.
256 devices in a mesh: energy: 32 (over x, y, core), cell: 8 (over z).
Axes of the slice: x: 4, y: 4, z: 8, core: 2. Of those that a mesh axis runs over, the one named last changes fastest.
Arguments:
- retarded_diag: bfloat16 [2, 64, 32, 256, 256], P(None, 'energy', 'cell'), may hold values from -0.375 to 0.375
- retarded_lower: bfloat16 [2, 64, 32, 256, 256], P(None, 'energy', 'cell'), may hold values from -0.375 to 0.375
- retarded_upper: bfloat16 [2, 64, 32, 256, 256], P(None, 'energy', 'cell'), may hold values from -0.375 to 0.375
- sigma_lesser: bfloat16 [2, 64, 32, 256, 256], P(None, 'energy', 'cell'), may hold values from -6 to 6
- screened: bfloat16 [2, 32, 128], P(None, 'cell'), may hold values from -0.5 to 0.5
- kept: int32 [32, 8], P('cell'), may hold values from 0 to 15, as said below
- kept_count: int32 [32], P('cell'), may hold values from 1 to 8, as said below
Outputs:
- sigma_new: bfloat16 [2, 64, 32, 8, 4096], P(None, 'energy', 'cell')
Inputs may be any that keep to these rules, and one draw needn't show every extreme that they name: `kept`: each row holds 8 different sub-block numbers. `kept_count`: some cell has 8 live slots and some other cell 1.
All inputs are finite; a program needn't handle non-finite values.
Results may differ from a plain program's by a relative error of at most 0.0057.
Values may be sent and summed in bfloat16 or wider, within the bound.
A program may use at most 128 MiB of HBM per device.

v0:
```python
from functools import partial
import jax
import jax.numpy as jnp
from jax import lax
from jax.sharding import PartitionSpec as P

ORB = 256
SUB = 64
KMAX = 8


def with_halo(block, sides, width):
    for axis, dim in sides:
        count = lax.axis_size(axis)
        forward = [(i, i + 1) for i in range(count - 1)]
        backward = [(target, source) for source, target in forward]
        low = lax.ppermute(
            lax.slice_in_dim(block, block.shape[dim] - width, None, axis=dim), axis, forward
        )
        high = lax.ppermute(lax.slice_in_dim(block, 0, width, axis=dim), axis, backward)
        block = jnp.concatenate([low, block, high], axis=dim)
    return block


def batched(left_side, right_side):
    return jnp.einsum("ecij,ecjk->ecik", left_side, right_side, preferred_element_type=jnp.float32)


def strips(hot, blocks):
    shaped = blocks.reshape(blocks.shape[0], blocks.shape[1], hot.shape[2], SUB, blocks.shape[3])
    return jnp.einsum("ckp,ecpij->eckij", hot, shaped, preferred_element_type=jnp.float32).astype(
        jnp.bfloat16
    )


def outer_part(left_side, right_side):
    return jnp.einsum(
        "eckij,eckqj->cekiq", left_side, right_side, preferred_element_type=jnp.float32
    )


def kept_sandwich(row_hot, col_hot, factor, middle):
    inner_r = (batched(factor[0], middle[0]) - batched(factor[1], middle[1])).astype(jnp.bfloat16)
    inner_i = (batched(factor[0], middle[1]) + batched(factor[1], middle[0])).astype(jnp.bfloat16)
    rows_r = strips(row_hot, inner_r)
    rows_i = strips(row_hot, inner_i)
    factor_r = strips(col_hot, factor[0])
    factor_i = strips(col_hot, factor[1])
    outer_r = outer_part(rows_r, factor_r) + outer_part(rows_i, factor_i)
    outer_i = outer_part(rows_i, factor_r) - outer_part(rows_r, factor_i)
    return (outer_r, outer_i)


def toeplitz(screened):
    energy_count = screened.shape[2] // 2
    position = jnp.arange(energy_count, dtype=jnp.int32)
    offsets = position[:, None] - position[None, :] + energy_count - 1
    return jnp.take(screened, offsets, axis=2)


def convolve(kernel, chosen):
    shape_in = chosen.shape
    flat = chosen.reshape(2, shape_in[1], shape_in[2], shape_in[3] * shape_in[4])
    form = "cef,cfm->cem"
    real_part = jnp.einsum(
        form, kernel[0], flat[0], preferred_element_type=jnp.float32
    ) - jnp.einsum(form, kernel[1], flat[1], preferred_element_type=jnp.float32)
    imag_part = jnp.einsum(
        form, kernel[0], flat[1], preferred_element_type=jnp.float32
    ) + jnp.einsum(form, kernel[1], flat[0], preferred_element_type=jnp.float32)
    return jnp.stack([real_part, imag_part]).astype(jnp.bfloat16).reshape(shape_in)


def per_device(
    retarded_diag, retarded_lower, retarded_upper, sigma_lesser, screened, kept, kept_count
):
    padded = with_halo(sigma_lesser, (("cell", 2),), 1)
    cell_count = sigma_lesser.shape[2]
    prev_cell = padded[:, :, 0:cell_count]
    next_cell = padded[:, :, 2 : cell_count + 2]
    per_side = ORB // SUB
    sides = jnp.arange(per_side, dtype=jnp.int32)
    row_hot = ((kept // per_side)[:, :, None] == sides[None, None, :]).astype(jnp.bfloat16)
    col_hot = ((kept % per_side)[:, :, None] == sides[None, None, :]).astype(jnp.bfloat16)
    first_r, first_i = kept_sandwich(row_hot, col_hot, retarded_diag, sigma_lesser)
    second_r, second_i = kept_sandwich(row_hot, col_hot, retarded_lower, prev_cell)
    third_r, third_i = kept_sandwich(row_hot, col_hot, retarded_upper, next_cell)
    lesser = jnp.stack([first_r + second_r + third_r, first_i + second_i + third_i]).astype(
        jnp.bfloat16
    )
    lesser = lesser.reshape(lesser.shape[:4] + (SUB * SUB,))
    live_slots = (jnp.arange(KMAX, dtype=jnp.int32)[None, :] < kept_count[:, None]).astype(
        jnp.bfloat16
    )
    chosen = lesser * live_slots[None, :, None, :, None]
    kernel = toeplitz(screened)
    mapper = partial(convolve, kernel)
    convolved = mapper(lax.all_to_all(chosen, "energy", split_axis=4, concat_axis=2, tiled=True))
    result = lax.all_to_all(convolved, "energy", split_axis=2, concat_axis=4, tiled=True)
    return jnp.swapaxes(result, 1, 2)


def solution(mesh):
    placed = (
        P(None, "energy", "cell", None, None),
        P(None, "energy", "cell", None, None),
        P(None, "energy", "cell", None, None),
        P(None, "energy", "cell", None, None),
        P(None, "cell", None),
        P("cell", None),
        P("cell"),
    )
    return jax.shard_map(
        per_device,
        mesh=mesh,
        in_specs=placed,
        out_specs=P(None, "energy", "cell", None, None),
        check_vma=False,
    )
```

profile of v0, /device:TPU:129, one launch (start us, length us, event | category | flops | bytes accessed | tf_op | source)
XLA Modules:
  0.0 209.8 jit_solution(11229530620356024958)
XLA Ops:
  0.0 1.4 fusion.119
  1.4 2.6 %collective-permute-start = (bf16[2,2,1,256,256]{4,3,2,1,0:T(8,128)(2,1)S(1)}, bf16[2,2,1,256,256]{4,3,2,1,0:T(8,128)(2,1)S(1)}, u32[]{:S(2)}, u32[]{:S(2)}) collective-permute-start(bf16[2,2,1,256,256]{4,3,2,1,0:T(8,128)(2,1)S(1)} %get-tuple-element.11), channel_id=1, source_target_pairs={{0,1},{1,2},{2,3},{3,4},{4,5},{5,6},{6,7},{8,9},{9,10},{10,11},{11... | collective-permute-start | bytes 1572872 | tf_op jit(solution)/shard_map/ppermute | solution.py:17
  4.1 4.0 %collective-permute-start.1 = (bf16[2,2,1,256,256]{4,3,2,1,0:T(8,128)(2,1)S(1)}, bf16[2,2,1,256,256]{4,3,2,1,0:T(8,128)(2,1)S(1)}, u32[]{:S(2)}, u32[]{:S(2)}) collective-permute-start(bf16[2,2,1,256,256]{4,3,2,1,0:T(8,128)(2,1)S(1)} %get-tuple-element.12), channel_id=1, source_target_pairs={{1,0},{2,1},{3,2},{4,3},{5,4},{6,5},{7,6},{9,8},{10,9},{11,10},{12... | collective-permute-start | bytes 1572872 | tf_op jit(solution)/shard_map/ppermute | solution.py:20
  8.1 1.7 fusion.58
  15.9 2.2 %fusion.24 = f32[4,2,8,64,64]{4,3,2,1,0:T(8,128)} fusion(bf16[2,4,8,64,256]{4,2,3,0,1:T(8,128)(2,1)S(1)} %convert_bitcast_fusion.8, bf16[2,4,8,64,256]{4,2,3,0,1:T(8,128)(2,1)S(1)} %convert_bitcast_fusion.11), kind=kOutput, calls=%fused_computation.45 | convolution fusion | flops 134217728 | bytes 5242880 | tf_op jit(solution)/shard_map/eckij,eckqj->cekiq/dot_general | solution.py:37
  22.8 1.1 convert_bitcast_fusion.2
  23.9 1.3 convert_bitcast_fusion
  28.1 2.1 %fusion = f32[4,2,8,64,64]{4,3,2,1,0:T(8,128)} fusion(bf16[2,4,8,64,256]{4,2,3,0,1:T(8,128)(2,1)S(1)} %convert_bitcast_fusion, bf16[2,4,8,64,256]{4,2,3,0,1:T(8,128)(2,1)S(1)} %convert_bitcast_fusion.3), kind=kOutput, calls=%fused_computation.21 | convolution fusion | flops 134217728 | bytes 5242880 | tf_op jit(solution)/shard_map/eckij,eckqj->cekiq/dot_general | solution.py:37
  32.4 2.1 %fusion.4 = f32[4,2,8,64,64]{4,3,2,1,0:T(8,128)} fusion(bf16[2,4,8,64,256]{4,2,3,0,1:T(8,128)(2,1)S(1)} %convert_bitcast_fusion.1, bf16[2,4,8,64,256]{4,2,3,0,1:T(8,128)(2,1)S(1)} %convert_bitcast_fusion.2), kind=kOutput, calls=%fused_computation.25 | convolution fusion | flops 134217728 | bytes 5242880 | tf_op jit(solution)/shard_map/eckij,eckqj->cekiq/dot_general | solution.py:37
  37.7 2.2 %fusion.12 = f32[4,2,8,64,64]{4,3,2,1,0:T(8,128)} fusion(bf16[2,4,8,64,256]{4,2,3,0,1:T(8,128)(2,1)S(1)} %convert_bitcast_fusion.4, bf16[2,4,8,64,256]{4,2,3,0,1:T(8,128)(2,1)S(1)} %convert_bitcast_fusion.7), kind=kOutput, calls=%fused_computation.33 | convolution fusion | flops 134217728 | bytes 5242880 | tf_op jit(solution)/shard_map/eckij,eckqj->cekiq/dot_general | solution.py:37
  42.0 2.4 %fusion.16 = f32[4,2,8,64,64]{4,3,2,1,0:T(8,128)} fusion(bf16[2,4,8,64,256]{4,2,3,0,1:T(8,128)(2,1)S(1)} %convert_bitcast_fusion.5, bf16[2,4,8,64,256]{4,2,3,0,1:T(8,128)(2,1)S(1)} %convert_bitcast_fusion.6), kind=kOutput, calls=%fused_computation.37 | convolution fusion | flops 134217728 | bytes 5242880 | tf_op jit(solution)/shard_map/eckij,eckqj->cekiq/dot_general | solution.py:37
  45.2 1.3 add_convert_fusion.1
  46.5 1.6 stack.18
  48.2 6.0 %add_convert_fusion = bf16[4,2,8,64,64]{4,3,2,1,0:T(8,128)(2,1)S(1)} fusion(f32[4,2,8,64,64]{4,3,2,1,0:T(8,128)} %fusion.4, f32[4,2,8,64,64]{4,3,2,1,0:T(8,128)} %fusion, f32[4,2,8,64,64]{4,3,2,1,0:T(8,128)} %fusion.16, f32[4,2,8,64,64]{4,3,2,1,0:T(8,128)} %fusion.12, f32[4,2,8,64,64]{4,3,2,1,0:T(8,128)} %fusion.24, ...), kind=kOutput, calls=%fused_computation.1 | convolution fusion | flops 135790592 | bytes 9961472 | tf_op jit(solution)/shard_map/eckij,eckqj->cekiq/dot_general | solution.py:37
  54.9 1.2 maximum_multiply_fusion
  56.1 28.1 %copy.169 = bf16[2,4,2,8,4096]{3,2,1,0,4:T(2,128)(2,1)} copy(bf16[2,4,2,8,4096]{4,3,2,1,0:T(8,128)(2,1)S(1)} %maximum_multiply_fusion) | data formatting | bytes 2097152 | tf_op jit(solution)/shard_map/mul | solution.py:95
  84.2 20.6 %reshape.121 = bf16[32,2,8192]{2,1,0:T(2,128)(2,1)} reshape(bf16[4096,2,4,2,8]{4,3,2,1,0:T(2,128)(2,1)} %bitcast.165) | data formatting | bytes 2097152
  104.8 8.5 %all-to-all-start = ((bf16[32,2,8192]{2,1,0:T(2,128)(2,1)}), bf16[32,2,8192]{2,1,0:T(2,128)(2,1)S(1)}, u32[]{:S(2)}, u32[]{:S(2)}) async-start(bf16[32,2,8192]{2,1,0:T(2,128)(2,1)} %reshape.121), calls=%async_computation | async-start | bytes 2097152 | tf_op jit(solution)/shard_map/all_to_all | solution.py:98
  113.6 13.8 %gather_fusion = bf16[4096,2,4]{2,1,0:T(2,128)(2,1)S(1)} fusion(bf16[2,4,128]{1,0,2:T(2,128)(2,1)S(1)} %copy.130, s32[4096]{0:T(1024)S(1)} %broadcast_clamp_fusion), kind=kCustom, calls=%fused_computation | custom fusion | bytes 147456 | tf_op jit(solution)/shard_map/jit(_take)/gather | solution.py:58
  127.3 1.8 copy.176
  130.2 20.8 %reshape.122 = bf16[4096,2,4,2,8]{4,3,2,1,0:T(2,128)(2,1)} reshape(bf16[32,2,8192]{2,1,0:T(2,128)(2,1)S(1)} %all-to-all-done) | data formatting | bytes 2097152
  151.0 32.1 %copy.170 = bf16[2,4,2,8,32,128]{5,3,2,4,1,0:T(8,128)(2,1)S(1)} copy(bf16[2,4,2,8,32,128]{3,2,1,0,5,4:T(2,128)(2,1)} %bitcast.166) | data formatting | bytes 2097152 | tf_op jit(solution)/shard_map/all_to_all | solution.py:98
  185.5 23.1 %all_to_all.33 = bf16[2,4,64,8,128]{4,3,1,0,2:T(8,128)(2,1)S(1)} all-to-all(bf16[2,4,64,8,128]{4,3,1,0,2:T(8,128)(2,1)S(1)} %copy.177), channel_id=1, replica_groups=mesh['energy'=32,'cell'=8] {'energy'}, dimensions={2} | all-to-all | bytes 2097152 | tf_op jit(solution)/shard_map/all_to_all | solution.py:99
  208.6 1.2 copy.262
  (71 shorter events, 26.1 us)
Async XLA Ops:
  0.0 8.1 %copy-start = (bf16[2,2,4,256,256]{4,3,2,1,0:T(8,128)(2,1)S(1)}, bf16[2,2,4,256,256]{4,3,2,1,0:T(8,128)(2,1)}, u32[]{:S(2)}) copy-start(bf16[2,2,4,256,256]{4,3,2,1,0:T(8,128)(2,1)} %param.10) | copy-start | bytes 6291460
  1.4 23.9 %collective-permute-start = (bf16[2,2,1,256,256]{4,3,2,1,0:T(8,128)(2,1)S(1)}, bf16[2,2,1,256,256]{4,3,2,1,0:T(8,128)(2,1)S(1)}, u32[]{:S(2)}, u32[]{:S(2)}) collective-permute-start(bf16[2,2,1,256,256]{4,3,2,1,0:T(8,128)(2,1)S(1)} %get-tuple-element.11), channel_id=1, source_target_pairs={{0,1},{1,2},{2,3},{3,4},{4,5},{5,6},{6,7},{8,9},{9,10},{10,11},{11... | collective-permute-start | bytes 1572872 | tf_op jit(solution)/shard_map/ppermute | solution.py:17
  4.1 5.7 %copy-start.1 = (bf16[2,2,4,256,256]{4,3,2,1,0:T(8,128)(2,1)S(1)}, bf16[2,2,4,256,256]{4,3,2,1,0:T(8,128)(2,1)}, u32[]{:S(2)}) copy-start(bf16[2,2,4,256,256]{4,3,2,1,0:T(8,128)(2,1)} %param.7) | copy-start | bytes 6291460
  4.1 21.7 %collective-permute-start.1 = (bf16[2,2,1,256,256]{4,3,2,1,0:T(8,128)(2,1)S(1)}, bf16[2,2,1,256,256]{4,3,2,1,0:T(8,128)(2,1)S(1)}, u32[]{:S(2)}, u32[]{:S(2)}) collective-permute-start(bf16[2,2,1,256,256]{4,3,2,1,0:T(8,128)(2,1)S(1)} %get-tuple-element.12), channel_id=1, source_target_pairs={{1,0},{2,1},{3,2},{4,3},{5,4},{6,5},{7,6},{9,8},{10,9},{11,10},{12... | collective-permute-start | bytes 1572872 | tf_op jit(solution)/shard_map/ppermute | solution.py:20
  10.2 0.7 copy-start.5
  12.7 5.4 %copy-start.4 = (bf16[2,4,8,64,256]{4,2,3,0,1:T(8,128)(2,1)}, bf16[2,4,8,64,256]{4,2,3,0,1:T(8,128)(2,1)S(1)}, u32[]{:S(2)}) copy-start(bf16[2,4,8,64,256]{4,2,3,0,1:T(8,128)(2,1)S(1)} %convert_bitcast_fusion.9) | copy-start | bytes 6291460
  18.1 1.6 copy-start.3
  21.0 1.6 copy-start.2
  23.9 1.3 copy-start.7
  104.8 8.6 %copy-start.6 = (bf16[2,4,128]{2,1,0:T(4,128)(2,1)S(1)}, bf16[2,4,128]{2,1,0:T(4,128)(2,1)}, u32[]{:S(2)}) copy-start(bf16[2,4,128]{2,1,0:T(4,128)(2,1)} %param.11) | copy-start | bytes 6148
  104.8 25.4 %all-to-all-start = ((bf16[32,2,8192]{2,1,0:T(2,128)(2,1)}), bf16[32,2,8192]{2,1,0:T(2,128)(2,1)S(1)}, u32[]{:S(2)}, u32[]{:S(2)}) async-start(bf16[32,2,8192]{2,1,0:T(2,128)(2,1)} %reshape.121), calls=%async_computation | async-start | bytes 2097152 | tf_op jit(solution)/shard_map/all_to_all | solution.py:98
where the time goes:
time: 211 us; the launch traced here: 210 us
  local copies, waits for them, and re-layouts  126 us (60%)
  matrix products  42.3 us (20%)
  blocking collectives  23.1 us (11%)
  starting transfers between devices  15.1 us (7%)
    unnamed x22, local copies, waits for them, and re-layouts  43.6 us
    all_to_all x1, local copies, waits for them, and re-layouts, per_device(): lax.all_to_all(chosen, 'energy', split_axis=4, concat_axis=2, tiled=True)  32.1 us
    mul x1, local copies, waits for them, and re-layouts, per_device(): chosen = lesser * live_slots[None, :, None, :, None]  28.1 us
    all_to_all x1, blocking collectives, per_device(): lax.all_to_all(convolved, 'energy', split_axis=2, concat_axis=4, tiled=True)  23.1 us
    dot_general x12, matrix products, outer_part(): jnp.einsum('eckij,eckqj->cekiq', left_side, right_side, preferred_element...  22.3 us
    gather x2, local copies, waits for them, and re-layouts, toeplitz(): return jnp.take(screened, offsets, axis=2)  15.6 us
    dot_general x12, matrix products, strips(): jnp.einsum('ckp,ecpij->eckij', hot, shaped, preferred_element_type=jnp.fl...  12.3 us
    all_to_all x1, starting transfers between devices, per_device(): lax.all_to_all(chosen, 'energy', split_axis=4, concat_axis=2, tiled=True)  8.46 us
  transfers between devices with their start and end apart: 3, of which 1 were waited for; matrix products, arithmetic and copies ran while one was open for 15% of the time, Pallas kernels for 0%

commit v1 on v0

--- a/solution.py
+++ b/solution.py
@@ -96,7 +96,12 @@
     kernel = toeplitz(screened)
     mapper = partial(convolve, kernel)
     convolved = mapper(lax.all_to_all(chosen, "energy", split_axis=4, concat_axis=2, tiled=True))
-    result = lax.all_to_all(convolved, "energy", split_axis=2, concat_axis=4, tiled=True)
+    result = jnp.concatenate(
+        jax.lax.all_to_all(
+            jnp.stack(jnp.split(convolved, jax.lax.axis_size("energy"), axis=2)), "energy", 0, 0
+        ),
+        axis=4,
+    )
     return jnp.swapaxes(result, 1, 2)
 
 

time: 211 us -> 212 us (level)
    unnamed x22 -> x54, local copies, waits for them, and re-layouts: 43.6 us -> 44.1 us
where the time goes in v1:
time: 212 us; the launch traced here: 210 us
  local copies, waits for them, and re-layouts  127 us (60%)
  matrix products  42.3 us (20%)
  blocking collectives  23.1 us (11%)
  starting transfers between devices  15.1 us (7%)
    unnamed x54, local copies, waits for them, and re-layouts  44.1 us
    all_to_all x1, local copies, waits for them, and re-layouts, per_device(): lax.all_to_all(chosen, 'energy', split_axis=4, concat_axis=2, tiled=True)  32.1 us
    mul x1, local copies, waits for them, and re-layouts, per_device(): chosen = lesser * live_slots[None, :, None, :, None]  28.1 us
    all_to_all x1, blocking collectives, per_device(): jax.lax.all_to_all(jnp.stack(jnp.split(convolved, jax.lax.axis_size('ener...  23.1 us
    dot_general x12, matrix products, outer_part(): jnp.einsum('eckij,eckqj->cekiq', left_side, right_side, preferred_element...  22.3 us
    gather x2, local copies, waits for them, and re-layouts, toeplitz(): return jnp.take(screened, offsets, axis=2)  15.6 us
    dot_general x12, matrix products, strips(): jnp.einsum('ckp,ecpij->eckij', hot, shaped, preferred_element_type=jnp.fl...  12.3 us
    all_to_all x1, starting transfers between devices, per_device(): lax.all_to_all(chosen, 'energy', split_axis=4, concat_axis=2, tiled=True)  8.46 us
  transfers between devices with their start and end apart: 3, of which 1 were waited for; matrix products, arithmetic and copies ran while one was open for 15% of the time, Pallas kernels for 0%

profile of v1, /device:TPU:129, one launch (start us, length us, event | category | flops | bytes accessed | tf_op | source)
XLA Modules:
  0.0 210.0 jit_solution(1053324509742026319)
XLA Ops:
  0.0 1.4 fusion.119
  1.4 2.6 %collective-permute-start = (bf16[2,2,1,256,256]{4,3,2,1,0:T(8,128)(2,1)S(1)}, bf16[2,2,1,256,256]{4,3,2,1,0:T(8,128)(2,1)S(1)}, u32[]{:S(2)}, u32[]{:S(2)}) collective-permute-start(bf16[2,2,1,256,256]{4,3,2,1,0:T(8,128)(2,1)S(1)} %get-tuple-element.11), channel_id=1, source_target_pairs={{0,1},{1,2},{2,3},{3,4},{4,5},{5,6},{6,7},{8,9},{9,10},{10,11},{11... | collective-permute-start | bytes 1572872 | tf_op jit(solution)/shard_map/ppermute | solution.py:17
  4.1 4.0 %collective-permute-start.1 = (bf16[2,2,1,256,256]{4,3,2,1,0:T(8,128)(2,1)S(1)}, bf16[2,2,1,256,256]{4,3,2,1,0:T(8,128)(2,1)S(1)}, u32[]{:S(2)}, u32[]{:S(2)}) collective-permute-start(bf16[2,2,1,256,256]{4,3,2,1,0:T(8,128)(2,1)S(1)} %get-tuple-element.12), channel_id=1, source_target_pairs={{1,0},{2,1},{3,2},{4,3},{5,4},{6,5},{7,6},{9,8},{10,9},{11,10},{12... | collective-permute-start | bytes 1572872 | tf_op jit(solution)/shard_map/ppermute | solution.py:20
  8.1 1.7 fusion.58
  15.9 2.2 %fusion.24 = f32[4,2,8,64,64]{4,3,2,1,0:T(8,128)} fusion(bf16[2,4,8,64,256]{4,2,3,0,1:T(8,128)(2,1)S(1)} %convert_bitcast_fusion.8, bf16[2,4,8,64,256]{4,2,3,0,1:T(8,128)(2,1)S(1)} %convert_bitcast_fusion.11), kind=kOutput, calls=%fused_computation.45 | convolution fusion | flops 134217728 | bytes 5242880 | tf_op jit(solution)/shard_map/eckij,eckqj->cekiq/dot_general | solution.py:37
  22.8 1.1 convert_bitcast_fusion.2
  23.9 1.3 convert_bitcast_fusion
  28.1 2.1 %fusion = f32[4,2,8,64,64]{4,3,2,1,0:T(8,128)} fusion(bf16[2,4,8,64,256]{4,2,3,0,1:T(8,128)(2,1)S(1)} %convert_bitcast_fusion, bf16[2,4,8,64,256]{4,2,3,0,1:T(8,128)(2,1)S(1)} %convert_bitcast_fusion.3), kind=kOutput, calls=%fused_computation.21 | convolution fusion | flops 134217728 | bytes 5242880 | tf_op jit(solution)/shard_map/eckij,eckqj->cekiq/dot_general | solution.py:37
  32.4 2.1 %fusion.4 = f32[4,2,8,64,64]{4,3,2,1,0:T(8,128)} fusion(bf16[2,4,8,64,256]{4,2,3,0,1:T(8,128)(2,1)S(1)} %convert_bitcast_fusion.1, bf16[2,4,8,64,256]{4,2,3,0,1:T(8,128)(2,1)S(1)} %convert_bitcast_fusion.2), kind=kOutput, calls=%fused_computation.25 | convolution fusion | flops 134217728 | bytes 5242880 | tf_op jit(solution)/shard_map/eckij,eckqj->cekiq/dot_general | solution.py:37
  37.7 2.2 %fusion.12 = f32[4,2,8,64,64]{4,3,2,1,0:T(8,128)} fusion(bf16[2,4,8,64,256]{4,2,3,0,1:T(8,128)(2,1)S(1)} %convert_bitcast_fusion.4, bf16[2,4,8,64,256]{4,2,3,0,1:T(8,128)(2,1)S(1)} %convert_bitcast_fusion.7), kind=kOutput, calls=%fused_computation.33 | convolution fusion | flops 134217728 | bytes 5242880 | tf_op jit(solution)/shard_map/eckij,eckqj->cekiq/dot_general | solution.py:37
  42.0 2.4 %fusion.16 = f32[4,2,8,64,64]{4,3,2,1,0:T(8,128)} fusion(bf16[2,4,8,64,256]{4,2,3,0,1:T(8,128)(2,1)S(1)} %convert_bitcast_fusion.5, bf16[2,4,8,64,256]{4,2,3,0,1:T(8,128)(2,1)S(1)} %convert_bitcast_fusion.6), kind=kOutput, calls=%fused_computation.37 | convolution fusion | flops 134217728 | bytes 5242880 | tf_op jit(solution)/shard_map/eckij,eckqj->cekiq/dot_general | solution.py:37
  45.2 1.3 add_convert_fusion.1
  46.5 1.6 stack.117
  48.2 6.0 %add_convert_fusion = bf16[4,2,8,64,64]{4,3,2,1,0:T(8,128)(2,1)S(1)} fusion(f32[4,2,8,64,64]{4,3,2,1,0:T(8,128)} %fusion.4, f32[4,2,8,64,64]{4,3,2,1,0:T(8,128)} %fusion, f32[4,2,8,64,64]{4,3,2,1,0:T(8,128)} %fusion.16, f32[4,2,8,64,64]{4,3,2,1,0:T(8,128)} %fusion.12, f32[4,2,8,64,64]{4,3,2,1,0:T(8,128)} %fusion.24, ...), kind=kOutput, calls=%fused_computation.1 | convolution fusion | flops 135790592 | bytes 9961472 | tf_op jit(solution)/shard_map/eckij,eckqj->cekiq/dot_general | solution.py:37
  54.9 1.2 maximum_multiply_fusion
  56.1 28.1 %copy.167 = bf16[2,4,2,8,4096]{3,2,1,0,4:T(2,128)(2,1)} copy(bf16[2,4,2,8,4096]{4,3,2,1,0:T(8,128)(2,1)S(1)} %maximum_multiply_fusion) | data formatting | bytes 2097152 | tf_op jit(solution)/shard_map/mul | solution.py:95
  84.2 20.6 %reshape.129 = bf16[32,2,8192]{2,1,0:T(2,128)(2,1)} reshape(bf16[4096,2,4,2,8]{4,3,2,1,0:T(2,128)(2,1)} %bitcast.292) | data formatting | bytes 2097152
  104.8 8.5 %all-to-all-start = ((bf16[32,2,8192]{2,1,0:T(2,128)(2,1)}), bf16[32,2,8192]{2,1,0:T(2,128)(2,1)S(1)}, u32[]{:S(2)}, u32[]{:S(2)}) async-start(bf16[32,2,8192]{2,1,0:T(2,128)(2,1)} %reshape.129), calls=%async_computation | async-start | bytes 2097152 | tf_op jit(solution)/shard_map/all_to_all | solution.py:98
  113.6 13.8 %gather_fusion = bf16[4096,2,4]{2,1,0:T(2,128)(2,1)S(1)} fusion(bf16[2,4,128]{1,0,2:T(2,128)(2,1)S(1)} %copy.128, s32[4096]{0:T(1024)S(1)} %broadcast_clamp_fusion), kind=kCustom, calls=%fused_computation | custom fusion | bytes 147456 | tf_op jit(solution)/shard_map/jit(_take)/gather | solution.py:58
  127.3 1.8 copy.172
  130.2 20.8 %reshape.130 = bf16[4096,2,4,2,8]{4,3,2,1,0:T(2,128)(2,1)} reshape(bf16[32,2,8192]{2,1,0:T(2,128)(2,1)S(1)} %all-to-all-done) | data formatting | bytes 2097152
  151.0 32.1 %copy.168 = bf16[2,4,2,8,32,128]{5,3,2,4,1,0:T(8,128)(2,1)S(1)} copy(bf16[2,4,2,8,32,128]{3,2,1,0,5,4:T(2,128)(2,1)} %bitcast.293) | data formatting | bytes 2097152 | tf_op jit(solution)/shard_map/all_to_all | solution.py:98
  185.8 23.1 %all_to_all.20 = bf16[32,2,4,2,8,128]{5,4,3,2,1,0:T(8,128)(2,1)S(1)} all-to-all(bf16[32,2,4,2,8,128]{5,4,3,2,1,0:T(8,128)(2,1)S(1)} %constant_dynamic-update-slice_fusion.6), channel_id=1, replica_groups=mesh['energy'=32,'cell'=8] {'energy'}, dimensions={0} | all-to-all | bytes 2097152 | tf_op jit(solution)/shard_map/all_to_all | solution.py:100
  208.9 1.1 copy_bitcast_fusion
  (103 shorter events, 26.3 us)
Async XLA Ops:
  0.0 8.1 %copy-start = (bf16[2,2,4,256,256]{4,3,2,1,0:T(8,128)(2,1)S(1)}, bf16[2,2,4,256,256]{4,3,2,1,0:T(8,128)(2,1)}, u32[]{:S(2)}) copy-start(bf16[2,2,4,256,256]{4,3,2,1,0:T(8,128)(2,1)} %param.10) | copy-start | bytes 6291460
  1.4 23.9 %collective-permute-start = (bf16[2,2,1,256,256]{4,3,2,1,0:T(8,128)(2,1)S(1)}, bf16[2,2,1,256,256]{4,3,2,1,0:T(8,128)(2,1)S(1)}, u32[]{:S(2)}, u32[]{:S(2)}) collective-permute-start(bf16[2,2,1,256,256]{4,3,2,1,0:T(8,128)(2,1)S(1)} %get-tuple-element.11), channel_id=1, source_target_pairs={{0,1},{1,2},{2,3},{3,4},{4,5},{5,6},{6,7},{8,9},{9,10},{10,11},{11... | collective-permute-start | bytes 1572872 | tf_op jit(solution)/shard_map/ppermute | solution.py:17
  4.1 5.7 %copy-start.1 = (bf16[2,2,4,256,256]{4,3,2,1,0:T(8,128)(2,1)S(1)}, bf16[2,2,4,256,256]{4,3,2,1,0:T(8,128)(2,1)}, u32[]{:S(2)}) copy-start(bf16[2,2,4,256,256]{4,3,2,1,0:T(8,128)(2,1)} %param.7) | copy-start | bytes 6291460
  4.1 21.7 %collective-permute-start.1 = (bf16[2,2,1,256,256]{4,3,2,1,0:T(8,128)(2,1)S(1)}, bf16[2,2,1,256,256]{4,3,2,1,0:T(8,128)(2,1)S(1)}, u32[]{:S(2)}, u32[]{:S(2)}) collective-permute-start(bf16[2,2,1,256,256]{4,3,2,1,0:T(8,128)(2,1)S(1)} %get-tuple-element.12), channel_id=1, source_target_pairs={{1,0},{2,1},{3,2},{4,3},{5,4},{6,5},{7,6},{9,8},{10,9},{11,10},{12... | collective-permute-start | bytes 1572872 | tf_op jit(solution)/shard_map/ppermute | solution.py:20
  10.2 0.7 copy-start.5
  12.7 5.4 %copy-start.4 = (bf16[2,4,8,64,256]{4,2,3,0,1:T(8,128)(2,1)}, bf16[2,4,8,64,256]{4,2,3,0,1:T(8,128)(2,1)S(1)}, u32[]{:S(2)}) copy-start(bf16[2,4,8,64,256]{4,2,3,0,1:T(8,128)(2,1)S(1)} %convert_bitcast_fusion.9) | copy-start | bytes 6291460
  18.1 1.6 copy-start.3
  21.0 1.6 copy-start.2
  23.9 1.3 copy-start.7
  104.8 8.6 %copy-start.6 = (bf16[2,4,128]{2,1,0:T(4,128)(2,1)S(1)}, bf16[2,4,128]{2,1,0:T(4,128)(2,1)}, u32[]{:S(2)}) copy-start(bf16[2,4,128]{2,1,0:T(4,128)(2,1)} %param.11) | copy-start | bytes 6148
  104.8 25.4 %all-to-all-start = ((bf16[32,2,8192]{2,1,0:T(2,128)(2,1)}), bf16[32,2,8192]{2,1,0:T(2,128)(2,1)S(1)}, u32[]{:S(2)}, u32[]{:S(2)}) async-start(bf16[32,2,8192]{2,1,0:T(2,128)(2,1)} %reshape.129), calls=%async_computation | async-start | bytes 2097152 | tf_op jit(solution)/shard_map/all_to_all | solution.py:98
